TPU v7x, 256 devices: a whole 4x4x8 slice. The times are simulated.
256 devices in a mesh: req: 16 (over x_hi, y, core), ctx: 16 (over x_lo, z).
Axes of the slice: x: 4 (x_hi: 2, x_lo: 2; x = x_hi * 2 + x_lo), y: 4, z: 8, core: 2. Of those that a mesh axis runs over, the one named last changes fastest.
Arguments:
- queries: bfloat16 [1024, 8192], P(('req', 'ctx')), parts along dimension 0, may hold values from -15 to 15
- new_keys: bfloat16 [1024, 512], P(('req', 'ctx')), parts along dimension 0, may hold values from -9 to 9
- new_values: bfloat16 [1024, 512], P(('req', 'ctx')), parts along dimension 0, may hold values from -6 to 6
- cache_keys: bfloat16 [524288, 512], P(('req', 'ctx')), parts along dimension 0, may hold values from -6 to 6
- cache_values: bfloat16 [524288, 512], P(('req', 'ctx')), parts along dimension 0, may hold values from -6 to 6
- cache_length: int32 [16], P('req'), parts along dimension 0, may hold values from 8192 to 32767
- page_table: int32 [4096], P('req'), parts along dimension 0, may hold values from 0 to 255, each once
Outputs:
- attended: bfloat16 [1024, 8192], P(('req', 'ctx')), parts along dimension 0
There are 16 independent parts, one for each index of `req`. A program takes and returns all parts, laid end to end along the dimension named above; each array names one. Nothing has to cross between parts.
Inputs may be any that keep to these rules, and one draw needn't show every extreme that they name: A permutation: logical page p lies in physical rows page_table[p] * 128 to page_table[p] * 128 + 127.
All inputs are finite; a program needn't handle non-finite values.
Results may differ from a plain program's by a relative error of at most 0.004.
Values may be sent and summed in bfloat16 or wider, within the bound.
No kernel may reach another device: no remote copies, remote signals or barrier semaphores. Data moves between devices by JAX's collectives and lax.ppermute only.
A program may use at most 64 MiB of HBM per device.

v0:
```python
import functools

import jax
import jax.numpy as jnp
from jax import lax
from jax.experimental import pallas as pl
from jax.experimental.pallas import tpu as pltpu
from jax.sharding import PartitionSpec as P


KVH = 4
HD = 128
PAGE = 128
ROWS = 4
GROUP = 16
HR = ROWS * GROUP
BLOCK = KVH * HR
PAYLOAD = BLOCK + 16
KEPT = BLOCK + 8
FLOOR = -1e30
NEWPAD = 16
SCALE2 = HD ** (-0.5) * 1.4426950408889634
NT = (((1,), (1,)), ((), ()))
NN = (((1,), (0,)), ((), ()))


def split3(x):
    hi = x.astype(jnp.bfloat16)
    rest = x - hi.astype(jnp.float32)
    mid = rest.astype(jnp.bfloat16)
    low = (rest - mid.astype(jnp.float32)).astype(jnp.bfloat16)
    return [hi.astype(jnp.float32), mid.astype(jnp.float32), low.astype(jnp.float32)]


def lse_tile(rows):
    row = lax.broadcasted_iota(jnp.int32, (16, HD), 0)
    tile = jnp.zeros((16, HD), jnp.float32)
    for j, x in enumerate(rows):
        for part, piece in enumerate(split3(x)):
            tile = jnp.where(row == 2 * part + j, jnp.broadcast_to(piece, (16, HD)), tile)
    return tile.astype(jnp.bfloat16)


def prep_kernel(device_ref, length_ref, table_ref, k_hbm, v_hbm, nk_ref, nv_ref, k_out, v_out, live_out, nk_out, nv_out, k_ref, v_ref, sems):
    pages = k_ref.shape[0] // PAGE
    pieces = sems.shape[0] // 2
    size = k_ref.shape[0] // pieces
    copies = []
    for src, dst, base in ((v_hbm, v_ref, 0), (k_hbm, k_ref, pieces)):
        for i in range(pieces):
            at = pl.ds(i * size, size)
            copies.append(pltpu.make_async_copy(src.at[at], dst.at[at], sems.at[base + i]))
            copies[-1].start()
    entries = table_ref.shape[1]
    slot = lax.broadcasted_iota(jnp.int32, (pages, entries), 0) + device_ref[0] * pages
    index = lax.broadcasted_iota(jnp.int32, (pages, entries), 1)
    hit = jnp.broadcast_to(table_ref[...], (pages, entries)) == slot
    logical = jnp.sum(jnp.where(hit, index, 0), axis=1, keepdims=True)
    first = jnp.min(logical, axis=0, keepdims=True)
    offset = lax.broadcasted_iota(jnp.int32, (PAGE, 1), 0)
    nk_out[...] = jnp.zeros_like(nk_out)
    nv_out[...] = jnp.zeros_like(nv_out)
    nk_out[0:ROWS, :] = nk_ref[...]
    nv_out[0:ROWS, :] = nv_ref[...]

    def live_of(s):
        return jnp.broadcast_to(logical[s:s + 1, :], (PAGE, 1)) * PAGE + offset < length_ref[0]

    for s in range(pages):
        if s % (pages // pieces) == 0:
            copies[s // (pages // pieces)].wait()
        rows = slice(s * PAGE, (s + 1) * PAGE)
        live = live_of(s)
        v_out[rows, :] = jnp.where(live, v_ref[rows, :].astype(jnp.float32), 0.0).astype(jnp.bfloat16)
        live_out[rows, :] = jnp.broadcast_to(jnp.where(live, 1.0, 0.0), (PAGE, HD)).astype(jnp.bfloat16)
    for copy in copies[pieces:]:
        copy.wait()
    spare = nk_ref[0:1, :].astype(jnp.float32)
    for s in range(pages):
        mine = logical[s:s + 1, :]
        use = (mine == first) & (mine * PAGE < length_ref[0])
        spare = jnp.where(use, k_ref[s * PAGE:s * PAGE + 1, :].astype(jnp.float32), spare)
    for s in range(pages):
        rows = slice(s * PAGE, (s + 1) * PAGE)
        k_out[rows, :] = jnp.where(live_of(s), k_ref[rows, :].astype(jnp.float32), spare).astype(jnp.bfloat16)


def attend_kernel(blocks, nin, zsize, device_ref, *refs):
    q_refs, (k_ref, v_ref, live_ref, nk_ref, nv_ref) = refs[:nin], refs[nin:nin + 5]
    keep_ref, send_ref = refs[-7:-5]
    scores, probs, tops = refs[-5:-3], refs[-3:-1], refs[-1]
    m_rows = len(blocks) * HR
    keys = k_ref.shape[0]
    chunk, tile = 256, 32
    chunks, tiles = keys // chunk, m_rows // tile
    device = device_ref[0]
    x, z = device // zsize, lax.rem(device, zsize)

    row = lax.broadcasted_iota(jnp.int32, (HR, NEWPAD), 0)
    col = lax.broadcasted_iota(jnp.int32, (HR, NEWPAD), 1)
    bias = []
    for _, _, (column, by) in blocks:
        origin = (x if column == 0 else 1 - x) * zsize + lax.rem(z + (by % zsize), zsize)
        ok = (col < ROWS) & (col + (device - origin) * ROWS <= (row & (ROWS - 1)))
        bias.append(jnp.where(ok, 0.0, FLOOR))
    bias = jnp.concatenate(bias, 0)
    ones = jnp.ones((NEWPAD, HD), jnp.bfloat16)
    at = lax.broadcasted_iota(jnp.int32, (HR, HD), 0)
    lane = lax.broadcasted_iota(jnp.int32, (HR, HD), 1)

    def lanes(g):
        return slice(g * HD, (g + 1) * HD)

    def rows(g):
        return slice(g * HR, (g + 1) * HR)

    def load(g):
        q = jnp.concatenate([q_refs[i][w, rows(g), :] for (i, w), _, _ in blocks], 0).astype(jnp.float32) * SCALE2
        hi = q.astype(jnp.bfloat16)
        low = (q - hi.astype(jnp.float32)).astype(jnp.bfloat16)
        q = jnp.concatenate([hi, low], 1)
        nk = nk_ref[:, lanes(g)]
        return q, lax.dot_general(q, jnp.concatenate([nk, nk], 1), NT, preferred_element_type=jnp.float32) + bias

    def qk(g, q, c):
        k = k_ref[c * chunk:(c + 1) * chunk, lanes(g)]
        scores[g % 2][:, c * chunk:(c + 1) * chunk] = lax.dot_general(q, jnp.concatenate([k, k], 1), NT, preferred_element_type=jnp.float32)

    def softmax(g, sn, t):
        part = slice(t * tile, (t + 1) * tile)
        buf = scores[g % 2]
        top = buf[part, 0:HD]
        for c in range(1, keys // HD):
            top = jnp.maximum(top, buf[part, c * HD:(c + 1) * HD])
        top = jnp.maximum(jnp.max(top, axis=1, keepdims=True), jnp.max(sn[part], axis=1, keepdims=True))
        wide = jnp.broadcast_to(top, (tile, HD))
        tops[part, :] = wide
        for c in range(keys // HD):
            probs[g % 2][part, c * HD:(c + 1) * HD] = jnp.exp2(buf[part, c * HD:(c + 1) * HD] - wide).astype(jnp.bfloat16)
        return jnp.exp2(sn[part] - top).astype(jnp.bfloat16)

    def pv(g, pn):
        value = jnp.concatenate([v_ref[:, lanes(g)], live_ref[...]], 1)
        acc = lax.dot_general(probs[g % 2][...], value, NN, preferred_element_type=jnp.float32)
        acc = acc + lax.dot_general(pn, jnp.concatenate([nv_ref[:, lanes(g)], ones], 1), NN, preferred_element_type=jnp.float32)
        total = acc[:, HD:]
        some = total > 0.0
        out = jnp.where(some, acc[:, :HD] / total, 0.0)
        lse = jnp.where(some, tops[...] + jnp.log2(total), FLOOR)
        eye = at + (g % 2) * HR == lane
        found = []
        for b, (_, place, (column, _)) in enumerate(blocks):
            if column == 0:
                keep_ref[place, rows(g), :] = out[b * HR:(b + 1) * HR]
            else:
                send_ref[place, rows(g), :] = out[b * HR:(b + 1) * HR].astype(jnp.bfloat16)
            found.append(jnp.sum(jnp.where(eye, lse[b * HR:(b + 1) * HR], 0.0), axis=0, keepdims=True))
        return found

    lse = []
    q, sn = load(0)
    for c in range(chunks):
        qk(0, q, c)
    for g in range(KVH):
        now = sn
        if g + 1 < KVH:
            q, sn = load(g + 1)
        pn = []
        for t in range(max(chunks, tiles)):
            if g + 1 < KVH and t < chunks:
                qk(g + 1, q, t)
            if t < tiles:
                pn.append(softmax(g, now, t))
        lse.append(pv(g, jnp.concatenate(pn, 0)))
    for b, (_, place, (column, _)) in enumerate(blocks):
        found = [lse[0][b] + lse[1][b], lse[2][b] + lse[3][b]]
        if column == 0:
            for j in range(2):
                keep_ref[place, BLOCK + j:BLOCK + j + 1, :] = found[j]
        else:
            send_ref[place, BLOCK:PAYLOAD, :] = lse_tile(found)


VM = pl.BlockSpec(memory_space=pltpu.VMEM)
SM = pl.BlockSpec(memory_space=pltpu.SMEM)


def limit(mib):
    return pltpu.CompilerParams(vmem_limit_bytes=mib << 20)


def prep(device, length, table, k, v, nk, nv):
    keys = k.shape[0]
    shapes = [k.shape, v.shape, (keys, HD), (NEWPAD, KVH * HD), (NEWPAD, KVH * HD)]
    hbm = pl.BlockSpec(memory_space=pltpu.HBM)
    return pl.pallas_call(
        prep_kernel,
        out_shape=[jax.ShapeDtypeStruct(s, jnp.bfloat16) for s in shapes],
        in_specs=[SM, SM, VM, hbm, hbm, VM, VM],
        out_specs=[VM] * 5,
        scratch_shapes=[pltpu.VMEM(k.shape, jnp.bfloat16), pltpu.VMEM(v.shape, jnp.bfloat16), pltpu.SemaphoreType.DMA((8,))],
        compiler_params=limit(48),
        cost_estimate=pl.CostEstimate(flops=4 * keys * KVH * HD, bytes_accessed=8 * keys * KVH * HD, transcendentals=0),
        name="prep",
    )(device, length, table, k, v, nk, nv)


def attend(zsize, device, arrays, blocks, store, total, before=None):
    keys = store[0].shape[0]
    m_rows = len(blocks) * HR
    kept = sum(column == 0 for _, _, (column, _) in blocks)
    extra = [] if before is None else [before]
    return pl.pallas_call(
        functools.partial(attend_kernel, blocks, len(arrays), zsize),
        out_shape=[jax.ShapeDtypeStruct((kept, KEPT, HD), jnp.float32), jax.ShapeDtypeStruct((total, PAYLOAD, HD), jnp.bfloat16)],
        in_specs=[SM] + [VM] * (len(arrays) + 5 + len(extra)),
        out_specs=[VM] * 2,
        scratch_shapes=[pltpu.VMEM((m_rows, keys), jnp.float32)] * 2 + [pltpu.VMEM((m_rows, keys), jnp.bfloat16)] * 2 + [pltpu.VMEM((m_rows, HD), jnp.float32)],
        input_output_aliases={6 + len(arrays): 1} if extra else {},
        compiler_params=limit(20),
        cost_estimate=pl.CostEstimate(flops=4 * m_rows * KVH * keys * HD, bytes_accessed=4 * keys * KVH * HD, transcendentals=m_rows * KVH * keys),
    )(device, *arrays, *store, *extra)


def columns(rows):
    row = lax.broadcasted_iota(jnp.int32, (HD, HD), 0)
    square = jnp.zeros((HD, HD), jnp.float32)
    for i, x in enumerate(rows):
        square = jnp.where(row == i, jnp.broadcast_to(x, (HD, HD)), square)
    return square.T


def lse_rows(ref):
    tile = ref[BLOCK:PAYLOAD, :].astype(jnp.float32)
    return [tile[j:j + 1] + (tile[2 + j:3 + j] + tile[4 + j:5 + j]) for j in range(2)]


def shares(rows):
    top = functools.reduce(jnp.maximum, rows)
    w = [jnp.exp2(r - top) for r in rows]
    total = functools.reduce(jnp.add, w)
    inv = 1.0 / total
    return [x * inv for x in w], top + jnp.log2(total)


def pair_kernel(counts, own, *refs):
    keeps, got_ref, outs = refs[:len(counts)], refs[len(counts)], refs[len(counts) + 1:]
    places = [(keep, i) for keep, n in zip(keeps, counts) for i in range(n)]
    rows, lses = [], []
    for p, (keep, i) in enumerate(places):
        theirs = lse_rows(got_ref.at[p])
        lses.append([])
        for j in range(2):
            w, lse = shares([keep[i, BLOCK + j:BLOCK + j + 1, :], theirs[j]])
            rows += w
            lses[-1].append(lse)
    cols = columns(rows)
    for p, (keep, i) in enumerate(places):
        for j in range(2):
            at, c = slice(j * HD, (j + 1) * HD), 4 * p + 2 * j
            acc = cols[:, c:c + 1] * keep[i, at, :] + cols[:, c + 1:c + 2] * got_ref[p, at, :].astype(jnp.float32)
            outs[p][at, :] = acc.astype(outs[p].dtype)
            if own and p == 0:
                outs[p][BLOCK + j:BLOCK + j + 1, :] = lses[p][j]
        if not (own and p == 0):
            outs[p][BLOCK:PAYLOAD, :] = lse_tile(lses[p])


def pair(keeps, got, own):
    counts = [k.shape[0] for k in keeps]
    shapes = [jax.ShapeDtypeStruct((PAYLOAD, HD), jnp.bfloat16)] * sum(counts)
    if own:
        shapes[0] = jax.ShapeDtypeStruct((KEPT, HD), jnp.float32)
    return pl.pallas_call(
        functools.partial(pair_kernel, counts, own),
        out_shape=shapes,
        in_specs=[VM] * (len(keeps) + 1),
        out_specs=[VM] * len(shapes),
        compiler_params=limit(4),
    )(*keeps, got)


def final_kernel(n, own_ref, *refs):
    parts, out_ref = refs[:n], refs[n]
    theirs = [lse_rows(p) for p in parts]
    for j in range(2):
        at = slice(j * HD, (j + 1) * HD)
        w, _ = shares([own_ref[BLOCK + j:BLOCK + j + 1, :]] + [t[j] for t in theirs])
        cols = columns(w)
        acc = cols[:, 0:1] * own_ref[at, :]
        for i, p in enumerate(parts):
            acc = acc + cols[:, i + 1:i + 2] * p[at, :].astype(jnp.float32)
        out_ref[at, :] = acc.astype(jnp.bfloat16)


def final(own, parts):
    return pl.pallas_call(
        functools.partial(final_kernel, len(parts)),
        out_shape=jax.ShapeDtypeStruct((BLOCK, HD), jnp.bfloat16),
        in_specs=[VM] * (1 + len(parts)),
        out_specs=VM,
        compiler_params=limit(4),
        name="final",
    )(own, *parts)


def local(queries, new_keys, new_values, cache_keys, cache_values, cache_length, page_table):
    zsize = lax.axis_size("ctx") // 2
    half = zsize // 2

    def zshift(x, by):
        return lax.ppermute(x, "ctx", [(i, (i // zsize) * zsize + (i % zsize + by) % zsize) for i in range(2 * zsize)])

    def xswap(x):
        return lax.ppermute(x, "ctx", [(i, (i + zsize) % (2 * zsize)) for i in range(2 * zsize)])

    def blocks_at(k, base):
        return [((i, w), (base if w else 0) + i, (w, by)) for i, by in ((0, -k), (1, k)) for w in range(2)]

    device = lax.axis_index("ctx").astype(jnp.int32).reshape(1)
    mine = queries.reshape(ROWS, KVH * GROUP, HD).transpose(1, 0, 2).reshape(BLOCK, HD)
    store = prep(device, cache_length, page_table.reshape(1, -1), cache_keys, cache_values, new_keys, new_values)
    swapped, store = lax.optimization_barrier((xswap(mine), store))
    both = jnp.stack([mine, swapped])

    near = 2 * half - 3
    run = functools.partial(attend, zsize, device)
    keeps = []
    keep, send = run([both], [((0, w), 0, (w, 0)) for w in range(2)], store, near)
    keeps.append(keep)
    up, down = both, both
    for k in range(1, half - 1):
        up, down, send = lax.optimization_barrier((zshift(up, 1), zshift(down, -1), send))
        keep, send = run([up, down], blocks_at(k, 2 * k - 1), store, near, send)
        keeps.append(keep)
    up, down, send = lax.optimization_barrier((zshift(up, 1), zshift(down, -1), send))
    far = (zshift(up[0:1], 1), zshift(down[1:2], -1))
    far_keep, far_send = run([up, down], blocks_at(half - 1, 0), store, 3)
    far, far_send = lax.optimization_barrier((far, far_send))
    last_keep, far_send = run(list(far), [((0, 0), 0, (0, half)), ((1, 0), 2, (1, half))], store, 3, far_send)

    got, far_got = xswap(send), xswap(far_send)
    own, *out = pair(keeps, got, True)
    far_out = pair([far_keep, last_keep], far_got, False)
    back = [zshift(far_out[2], half), zshift(far_out[0], 1 - half), zshift(far_out[1], half - 1)]
    for k in range(half - 2, 0, -1):
        back += [zshift(out[2 * k - 2], -k), zshift(out[2 * k - 1], k)]
    out = final(own, back)
    return out.reshape(KVH * GROUP, ROWS, HD).transpose(1, 0, 2).reshape(ROWS, KVH * GROUP * HD)


def solution(mesh):
    spec = P(("req", "ctx"), None)
    in_specs = (spec, spec, spec, spec, spec, P("req"), P("req"))

    return jax.shard_map(local, mesh=mesh, in_specs=in_specs, out_specs=spec, check_vma=False)
```

profile of v0, /device:TPU:2, one launch (start us, length us, event | category | flops | bytes accessed | tf_op | source)
XLA Modules:
  0.0 67.3 jit_solution(16878804420247370489)
XLA Ops:
  0.0 2.2 %collective-permute-start = (bf16[256,128]{1,0:T(8,128)(2,1)}, bf16[256,128]{1,0:T(8,128)(2,1)S(1)}, u32[]{:S(2)}, u32[]{:S(2)}) collective-permute-start(bf16[256,128]{1,0:T(8,128)(2,1)} %bitcast.16), channel_id=1, source_target_pairs={{0,8},{1,9},{2,10},{3,11},{4,12},{5,13},{6,14},{7,15},{8,0},{9,1},... | collective-permute-start | bytes 196616 | tf_op jit(solution)/shard_map/ppermute | solution.py:315
  5.0 2.7 %prep.1 = (bf16[2048,512]{1,0:T(8,128)(2,1)S(1)}, bf16[2048,512]{1,0:T(8,128)(2,1)S(1)}, bf16[2048,128]{1,0:T(8,128)(2,1)S(1)}, bf16[16,512]{1,0:T(8,128)(2,1)S(1)}, bf16[16,512]{1,0:T(8,128)(2,1)S(1)}) custom-call(s32[1]{0:T(128)} %bitcast.device_ref, s32[1]{0:T(128)S(6)} %copy.16.length_ref, s32[1,256]{1,0:T(1,128)S(1)} %bitcast.15, ...), custom_call_target="tpu_custom_call" | custom-call | flops 4194304 | bytes 8388608 | tf_op jit(solution)/shard_map/prep/pallas_call | solution.py:196
  7.9 4.0 %collective-permute-start.2 = (bf16[2,256,128]{2,1,0:T(8,128)(2,1)S(1)}, bf16[2,256,128]{2,1,0:T(8,128)(2,1)S(1)}, u32[]{:S(2)}, u32[]{:S(2)}) collective-permute-start(bf16[2,256,128]{2,1,0:T(8,128)(2,1)S(1)} %pad_maximum_fusion.refs_0_), channel_id=1, source_target_pairs={{0,7},{1,0},{2,1},{3,2},{4,3},{5,4},{6,5},{7,6},{8,15},{9,8},{10,9... | collective-permute-start | bytes 393224 | tf_op jit(solution)/shard_map/ppermute | solution.py:312
  12.0 2.2 %shard_map.73 = (f32[1,264,128]{2,1,0:T(8,128)S(1)}, bf16[5,272,128]{2,1,0:T(8,128)(2,1)S(1)}) custom-call(s32[1]{0:T(128)} %bitcast.device_ref, bf16[2,256,128]{2,1,0:T(8,128)(2,1)S(1)} %pad_maximum_fusion.refs_0_, bf16[2048,512]{1,0:T(8,128)(2,1)S(1)} %get-tuple-element.52.refs_1_.refs_2_, bf16[2048,512]{1,0:T(8,128)(2,1)S(1)} %get-tuple-element.53.refs_2_.refs_3_, ...), custom_call_target="tpu_custom_call" | custom-call | flops 536870912 | bytes 4194304 | tf_op jit(solution)/shard_map/pallas_call | solution.py:213
  14.2 0.9 %collective-permute-done.1.refs_0_ = bf16[2,256,128]{2,1,0:T(8,128)(2,1)S(1)} collective-permute-done((bf16[2,256,128]{2,1,0:T(8,128)(2,1)S(1)}, bf16[2,256,128]{2,1,0:T(8,128)(2,1)S(1)}, u32[]{:S(2)}, u32[]{:S(2)}) %collective-permute-start.1) | collective-permute-done | bytes 131104 | tf_op jit(solution)/shard_map/ppermute | solution.py:312
  15.1 3.2 %collective-permute-start.4 = (bf16[2,256,128]{2,1,0:T(8,128)(2,1)S(1)}, bf16[2,256,128]{2,1,0:T(8,128)(2,1)S(1)}, u32[]{:S(2)}, u32[]{:S(2)}) collective-permute-start(bf16[2,256,128]{2,1,0:T(8,128)(2,1)S(1)} %collective-permute-done.2.refs_1_), channel_id=1, source_target_pairs={{0,7},{1,0},{2,1},{3,2},{4,3},{5,4},{6,5},{7,6},{8,15},{9,8},{10,9... | collective-permute-start | bytes 393224 | tf_op jit(solution)/shard_map/ppermute | solution.py:312
  18.3 2.9 %shard_map.74 = (f32[2,264,128]{2,1,0:T(8,128)S(1)}, bf16[5,272,128]{2,1,0:T(8,128)(2,1)S(1)}) custom-call(s32[1]{0:T(128)} %bitcast.device_ref, bf16[2,256,128]{2,1,0:T(8,128)(2,1)S(1)} %collective-permute-done.1.refs_0_, bf16[2,256,128]{2,1,0:T(8,128)(2,1)S(1)} %collective-permute-done.2.refs_1_, ...), custom_call_target="tpu_custom_call", output_to_operand_aliasing={{1}: (8, {})} | custom-call | flops 1073741824 | bytes 4194304 | tf_op jit(solution)/shard_map/pallas_call | solution.py:213
  21.3 2.7 %collective-permute-start.5 = (bf16[2,256,128]{2,1,0:T(8,128)(2,1)S(1)}, bf16[2,256,128]{2,1,0:T(8,128)(2,1)S(1)}, u32[]{:S(2)}, u32[]{:S(2)}) collective-permute-start(bf16[2,256,128]{2,1,0:T(8,128)(2,1)S(1)} %collective-permute-done.3.refs_0_), channel_id=1, source_target_pairs={{0,1},{1,2},{2,3},{3,4},{4,5},{5,6},{6,7},{7,0},{8,9},{9,10},{10,1... | collective-permute-start | bytes 393224 | tf_op jit(solution)/shard_map/ppermute | solution.py:312
  24.6 2.9 %shard_map.75 = (f32[2,264,128]{2,1,0:T(8,128)S(1)}, bf16[5,272,128]{2,1,0:T(8,128)(2,1)S(1)}) custom-call(s32[1]{0:T(128)} %bitcast.device_ref, bf16[2,256,128]{2,1,0:T(8,128)(2,1)S(1)} %collective-permute-done.3.refs_0_, bf16[2,256,128]{2,1,0:T(8,128)(2,1)S(1)} %collective-permute-done.4.refs_1_, ...), custom_call_target="tpu_custom_call", output_to_operand_aliasing={{1}: (8, {})} | custom-call | flops 1073741824 | bytes 4194304 | tf_op jit(solution)/shard_map/pallas_call | solution.py:213
  27.5 1.5 %collective-permute-done.6.refs_1_ = bf16[2,256,128]{2,1,0:T(8,128)(2,1)S(1)} collective-permute-done((bf16[2,256,128]{2,1,0:T(8,128)(2,1)S(1)}, bf16[2,256,128]{2,1,0:T(8,128)(2,1)S(1)}, u32[]{:S(2)}, u32[]{:S(2)}) %collective-permute-start.6) | collective-permute-done | bytes 131104 | tf_op jit(solution)/shard_map/ppermute | solution.py:312
  29.0 1.5 %collective-permute-start.7 = (bf16[5,272,128]{2,1,0:T(8,128)(2,1)S(1)}, bf16[5,272,128]{2,1,0:T(8,128)(2,1)S(1)}, u32[]{:S(2)}, u32[]{:S(2)}) collective-permute-start(bf16[5,272,128]{2,1,0:T(8,128)(2,1)S(1)} %get-tuple-element.69), channel_id=1, source_target_pairs={{0,8},{1,9},{2,10},{3,11},{4,12},{5,13},{6,14},{7,15},{8,0},{9,1},... | collective-permute-start | bytes 1044488 | tf_op jit(solution)/shard_map/ppermute | solution.py:315
  30.5 2.3 %collective-permute-start.8 = (bf16[1,256,128]{2,1,0:T(8,128)(2,1)S(1)}, bf16[1,256,128]{2,1,0:T(8,128)(2,1)S(1)}, u32[]{:S(2)}, u32[]{:S(2)}) collective-permute-start(bf16[1,256,128]{2,1,0:T(8,128)(2,1)S(1)} %slice.6), channel_id=1, source_target_pairs={{0,1},{1,2},{2,3},{3,4},{4,5},{5,6},{6,7},{7,0},{8,9},{9,10},{10,1... | collective-permute-start | bytes 196616 | tf_op jit(solution)/shard_map/ppermute | solution.py:312
  32.8 1.0 %collective-permute-start.9 = (bf16[1,256,128]{2,1,0:T(8,128)(2,1)S(1)}, bf16[1,256,128]{2,1,0:T(8,128)(2,1)S(1)}, u32[]{:S(2)}, u32[]{:S(2)}) collective-permute-start(bf16[1,256,128]{2,1,0:T(8,128)(2,1)S(1)} %slice.7), channel_id=1, source_target_pairs={{0,7},{1,0},{2,1},{3,2},{4,3},{5,4},{6,5},{7,6},{8,15},{9,8},{10,9... | collective-permute-start | bytes 196616 | tf_op jit(solution)/shard_map/ppermute | solution.py:312
  33.7 2.9 %shard_map.77 = (f32[2,264,128]{2,1,0:T(8,128)S(1)}, bf16[3,272,128]{2,1,0:T(8,128)(2,1)S(1)}) custom-call(s32[1]{0:T(128)} %bitcast.device_ref, bf16[2,256,128]{2,1,0:T(8,128)(2,1)S(1)} %collective-permute-done.5.refs_0_, bf16[2,256,128]{2,1,0:T(8,128)(2,1)S(1)} %collective-permute-done.6.refs_1_, bf16[2048,512]{1,0:T(8,128)(2,1)S(1)} %get-tuple-element.52.refs_1_.refs_2_, ...), custom_call_target="tpu_custom_call" | custom-call | flops 1073741824 | bytes 4194304 | tf_op jit(solution)/shard_map/pallas_call | solution.py:213
  37.0 2.2 %shard_map.78 = (f32[1,264,128]{2,1,0:T(8,128)S(1)}, bf16[3,272,128]{2,1,0:T(8,128)(2,1)S(1)}) custom-call(s32[1]{0:T(128)} %bitcast.device_ref, bf16[1,256,128]{2,1,0:T(8,128)(2,1)S(1)} %collective-permute-done.8.refs_0_, bf16[1,256,128]{2,1,0:T(8,128)(2,1)S(1)} %collective-permute-done.9.refs_1_, ...), custom_call_target="tpu_custom_call", output_to_operand_aliasing={{1}: (8, {})} | custom-call | flops 536870912 | bytes 4194304 | tf_op jit(solution)/shard_map/pallas_call | solution.py:213
  39.7 5.5 %collective-permute-done.10.refs_2_ = bf16[3,272,128]{2,1,0:T(8,128)(2,1)S(1)} collective-permute-done((bf16[3,272,128]{2,1,0:T(8,128)(2,1)S(1)}, bf16[3,272,128]{2,1,0:T(8,128)(2,1)S(1)}, u32[]{:S(2)}, u32[]{:S(2)}) %collective-permute-start.10) | collective-permute-done | bytes 208928 | tf_op jit(solution)/shard_map/ppermute | solution.py:315
  45.6 2.7 %collective-permute-start.11 = (bf16[272,128]{1,0:T(8,128)(2,1)S(1)}, bf16[272,128]{1,0:T(8,128)(2,1)S(1)}, u32[]{:S(2)}, u32[]{:S(2)}) collective-permute-start(bf16[272,128]{1,0:T(8,128)(2,1)S(1)} %get-tuple-element.80), channel_id=1, source_target_pairs={{0,4},{1,5},{2,6},{3,7},{4,0},{5,1},{6,2},{7,3},{8,12},{9,13},{10,... | collective-permute-start | bytes 208904 | tf_op jit(solution)/shard_map/ppermute | solution.py:312
  48.3 2.9 %collective-permute-start.12 = (bf16[272,128]{1,0:T(8,128)(2,1)S(1)}, bf16[272,128]{1,0:T(8,128)(2,1)S(1)}, u32[]{:S(2)}, u32[]{:S(2)}) collective-permute-start(bf16[272,128]{1,0:T(8,128)(2,1)S(1)} %get-tuple-element.81), channel_id=1, source_target_pairs={{0,5},{1,6},{2,7},{3,0},{4,1},{5,2},{6,3},{7,4},{8,13},{9,14},{10,... | collective-permute-start | bytes 208904 | tf_op jit(solution)/shard_map/ppermute | solution.py:312
  51.1 1.0 %collective-permute-start.13 = (bf16[272,128]{1,0:T(8,128)(2,1)S(1)}, bf16[272,128]{1,0:T(8,128)(2,1)S(1)}, u32[]{:S(2)}, u32[]{:S(2)}) collective-permute-start(bf16[272,128]{1,0:T(8,128)(2,1)S(1)} %get-tuple-element.82), channel_id=1, source_target_pairs={{0,3},{1,4},{2,5},{3,6},{4,7},{5,0},{6,1},{7,2},{8,11},{9,12},{10,... | collective-permute-start | bytes 208904 | tf_op jit(solution)/shard_map/ppermute | solution.py:312
  52.7 4.0 %collective-permute-start.14 = (bf16[272,128]{1,0:T(8,128)(2,1)S(1)}, bf16[272,128]{1,0:T(8,128)(2,1)S(1)}, u32[]{:S(2)}, u32[]{:S(2)}) collective-permute-start(bf16[272,128]{1,0:T(8,128)(2,1)S(1)} %get-tuple-element.83), channel_id=1, source_target_pairs={{0,6},{1,7},{2,0},{3,1},{4,2},{5,3},{6,4},{7,5},{8,14},{9,15},{10,... | collective-permute-start | bytes 208904 | tf_op jit(solution)/shard_map/ppermute | solution.py:312
  56.7 4.0 %collective-permute-start.16 = (bf16[272,128]{1,0:T(8,128)(2,1)S(1)}, bf16[272,128]{1,0:T(8,128)(2,1)S(1)}, u32[]{:S(2)}, u32[]{:S(2)}) collective-permute-start(bf16[272,128]{1,0:T(8,128)(2,1)S(1)} %get-tuple-element.85), channel_id=1, source_target_pairs={{0,7},{1,0},{2,1},{3,2},{4,3},{5,4},{6,5},{7,6},{8,15},{9,8},{10,9... | collective-permute-start | bytes 208904 | tf_op jit(solution)/shard_map/ppermute | solution.py:312
  60.7 3.0 %collective-permute-done.15.refs_4_ = bf16[272,128]{1,0:T(8,128)(2,1)S(1)} collective-permute-done((bf16[272,128]{1,0:T(8,128)(2,1)S(1)}, bf16[272,128]{1,0:T(8,128)(2,1)S(1)}, u32[]{:S(2)}, u32[]{:S(2)}) %collective-permute-start.15) | collective-permute-done | bytes 69664 | tf_op jit(solution)/shard_map/ppermute | solution.py:312
  63.7 2.5 %collective-permute-done.17.refs_6_ = bf16[272,128]{1,0:T(8,128)(2,1)S(1)} collective-permute-done((bf16[272,128]{1,0:T(8,128)(2,1)S(1)}, bf16[272,128]{1,0:T(8,128)(2,1)S(1)}, u32[]{:S(2)}, u32[]{:S(2)}) %collective-permute-start.17) | collective-permute-done | bytes 69664 | tf_op jit(solution)/shard_map/ppermute | solution.py:312
  66.2 1.1 %final.1 = bf16[256,128]{1,0:T(8,128)(2,1)} custom-call(f32[264,128]{1,0:T(8,128)S(1)} %get-tuple-element.70.own_ref, bf16[272,128]{1,0:T(8,128)(2,1)S(1)} %collective-permute-done.11.refs_0_, bf16[272,128]{1,0:T(8,128)(2,1)S(1)} %collective-permute-done.12.refs_1_, bf16[272,128]{1,0:T(8,128)(2,1)S(1)} %collective-permute-done.13.refs_2_, ...), custom_call_target="tpu_custom_call" | custom-call | tf_op jit(solution)/shard_map/final/pallas_call | solution.py:297
  (32 shorter events, 4.8 us)
Async XLA Ops:
  0.0 7.6 %collective-permute-start = (bf16[256,128]{1,0:T(8,128)(2,1)}, bf16[256,128]{1,0:T(8,128)(2,1)S(1)}, u32[]{:S(2)}, u32[]{:S(2)}) collective-permute-start(bf16[256,128]{1,0:T(8,128)(2,1)} %bitcast.16), channel_id=1, source_target_pairs={{0,8},{1,9},{2,10},{3,11},{4,12},{5,13},{6,14},{7,15},{8,0},{9,1},... | collective-permute-start | bytes 196616 | tf_op jit(solution)/shard_map/ppermute | solution.py:315
  2.9 0.7 %copy-start = (bf16[4,512]{1,0:T(4,128)(2,1)S(1)}, bf16[4,512]{1,0:T(4,128)(2,1)}, u32[]{:S(2)}) copy-start(bf16[4,512]{1,0:T(4,128)(2,1)} %nk_ref.1) | copy-start | bytes 12292
  3.6 0.7 %copy-start.1 = (bf16[4,512]{1,0:T(4,128)(2,1)S(1)}, bf16[4,512]{1,0:T(4,128)(2,1)}, u32[]{:S(2)}) copy-start(bf16[4,512]{1,0:T(4,128)(2,1)} %nv_ref.1) | copy-start | bytes 12292
  4.3 0.7 %copy-start.2 = (s32[256]{0:T(256)S(1)}, s32[256]{0:T(256)}, u32[]{:S(2)}) copy-start(s32[256]{0:T(256)} %param.13) | copy-start | bytes 3076
  4.9 2.7 %copy-start.3 = (bf16[4,8192]{1,0:T(4,128)(2,1)S(1)}, bf16[4,8192]{1,0:T(4,128)(2,1)}, u32[]{:S(2)}) copy-start(bf16[4,8192]{1,0:T(4,128)(2,1)} %param.7) | copy-start | bytes 196612
  7.7 7.4 %collective-permute-start.1 = (bf16[2,256,128]{2,1,0:T(8,128)(2,1)S(1)}, bf16[2,256,128]{2,1,0:T(8,128)(2,1)S(1)}, u32[]{:S(2)}, u32[]{:S(2)}) collective-permute-start(bf16[2,256,128]{2,1,0:T(8,128)(2,1)S(1)} %pad_maximum_fusion.refs_0_), channel_id=1, source_target_pairs={{0,1},{1,2},{2,3},{3,4},{4,5},{5,6},{6,7},{7,0},{8,9},{9,10},{10,1... | collective-permute-start | bytes 393224 | tf_op jit(solution)/shard_map/ppermute | solution.py:312
  7.9 7.2 %collective-permute-start.2 = (bf16[2,256,128]{2,1,0:T(8,128)(2,1)S(1)}, bf16[2,256,128]{2,1,0:T(8,128)(2,1)S(1)}, u32[]{:S(2)}, u32[]{:S(2)}) collective-permute-start(bf16[2,256,128]{2,1,0:T(8,128)(2,1)S(1)} %pad_maximum_fusion.refs_0_), channel_id=1, source_target_pairs={{0,7},{1,0},{2,1},{3,2},{4,3},{5,4},{6,5},{7,6},{8,15},{9,8},{10,9... | collective-permute-start | bytes 393224 | tf_op jit(solution)/shard_map/ppermute | solution.py:312
  15.1 6.2 %collective-permute-start.3 = (bf16[2,256,128]{2,1,0:T(8,128)(2,1)S(1)}, bf16[2,256,128]{2,1,0:T(8,128)(2,1)S(1)}, u32[]{:S(2)}, u32[]{:S(2)}) collective-permute-start(bf16[2,256,128]{2,1,0:T(8,128)(2,1)S(1)} %collective-permute-done.1.refs_0_), channel_id=1, source_target_pairs={{0,1},{1,2},{2,3},{3,4},{4,5},{5,6},{6,7},{7,0},{8,9},{9,10},{10,1... | collective-permute-start | bytes 393224 | tf_op jit(solution)/shard_map/ppermute | solution.py:312
  15.1 6.2 %collective-permute-start.4 = (bf16[2,256,128]{2,1,0:T(8,128)(2,1)S(1)}, bf16[2,256,128]{2,1,0:T(8,128)(2,1)S(1)}, u32[]{:S(2)}, u32[]{:S(2)}) collective-permute-start(bf16[2,256,128]{2,1,0:T(8,128)(2,1)S(1)} %collective-permute-done.2.refs_1_), channel_id=1, source_target_pairs={{0,7},{1,0},{2,1},{3,2},{4,3},{5,4},{6,5},{7,6},{8,15},{9,8},{10,9... | collective-permute-start | bytes 393224 | tf_op jit(solution)/shard_map/ppermute | solution.py:312
  21.3 6.3 %collective-permute-start.5 = (bf16[2,256,128]{2,1,0:T(8,128)(2,1)S(1)}, bf16[2,256,128]{2,1,0:T(8,128)(2,1)S(1)}, u32[]{:S(2)}, u32[]{:S(2)}) collective-permute-start(bf16[2,256,128]{2,1,0:T(8,128)(2,1)S(1)} %collective-permute-done.3.refs_0_), channel_id=1, source_target_pairs={{0,1},{1,2},{2,3},{3,4},{4,5},{5,6},{6,7},{7,0},{8,9},{9,10},{10,1... | collective-permute-start | bytes 393224 | tf_op jit(solution)/shard_map/ppermute | solution.py:312
  24.0 5.0 %collective-permute-start.6 = (bf16[2,256,128]{2,1,0:T(8,128)(2,1)S(1)}, bf16[2,256,128]{2,1,0:T(8,128)(2,1)S(1)}, u32[]{:S(2)}, u32[]{:S(2)}) collective-permute-start(bf16[2,256,128]{2,1,0:T(8,128)(2,1)S(1)} %collective-permute-done.4.refs_1_), channel_id=1, source_target_pairs={{0,7},{1,0},{2,1},{3,2},{4,3},{5,4},{6,5},{7,6},{8,15},{9,8},{10,9... | collective-permute-start | bytes 393224 | tf_op jit(solution)/shard_map/ppermute | solution.py:312
  29.0 23.1 %collective-permute-start.7 = (bf16[5,272,128]{2,1,0:T(8,128)(2,1)S(1)}, bf16[5,272,128]{2,1,0:T(8,128)(2,1)S(1)}, u32[]{:S(2)}, u32[]{:S(2)}) collective-permute-start(bf16[5,272,128]{2,1,0:T(8,128)(2,1)S(1)} %get-tuple-element.69), channel_id=1, source_target_pairs={{0,8},{1,9},{2,10},{3,11},{4,12},{5,13},{6,14},{7,15},{8,0},{9,1},... | collective-permute-start | bytes 1044488 | tf_op jit(solution)/shard_map/ppermute | solution.py:315
  30.5 6.2 %collective-permute-start.8 = (bf16[1,256,128]{2,1,0:T(8,128)(2,1)S(1)}, bf16[1,256,128]{2,1,0:T(8,128)(2,1)S(1)}, u32[]{:S(2)}, u32[]{:S(2)}) collective-permute-start(bf16[1,256,128]{2,1,0:T(8,128)(2,1)S(1)} %slice.6), channel_id=1, source_target_pairs={{0,1},{1,2},{2,3},{3,4},{4,5},{5,6},{6,7},{7,0},{8,9},{9,10},{10,1... | collective-permute-start | bytes 196616 | tf_op jit(solution)/shard_map/ppermute | solution.py:312
  32.8 4.3 %collective-permute-start.9 = (bf16[1,256,128]{2,1,0:T(8,128)(2,1)S(1)}, bf16[1,256,128]{2,1,0:T(8,128)(2,1)S(1)}, u32[]{:S(2)}, u32[]{:S(2)}) collective-permute-start(bf16[1,256,128]{2,1,0:T(8,128)(2,1)S(1)} %slice.7), channel_id=1, source_target_pairs={{0,7},{1,0},{2,1},{3,2},{4,3},{5,4},{6,5},{7,6},{8,15},{9,8},{10,9... | collective-permute-start | bytes 196616 | tf_op jit(solution)/shard_map/ppermute | solution.py:312
  39.3 5.9 %collective-permute-start.10 = (bf16[3,272,128]{2,1,0:T(8,128)(2,1)S(1)}, bf16[3,272,128]{2,1,0:T(8,128)(2,1)S(1)}, u32[]{:S(2)}, u32[]{:S(2)}) collective-permute-start(bf16[3,272,128]{2,1,0:T(8,128)(2,1)S(1)} %get-tuple-element.79), channel_id=1, source_target_pairs={{0,8},{1,9},{2,10},{3,11},{4,12},{5,13},{6,14},{7,15},{8,0},{9,1},... | collective-permute-start | bytes 626696 | tf_op jit(solution)/shard_map/ppermute | solution.py:315
  45.6 11.1 %collective-permute-start.11 = (bf16[272,128]{1,0:T(8,128)(2,1)S(1)}, bf16[272,128]{1,0:T(8,128)(2,1)S(1)}, u32[]{:S(2)}, u32[]{:S(2)}) collective-permute-start(bf16[272,128]{1,0:T(8,128)(2,1)S(1)} %get-tuple-element.80), channel_id=1, source_target_pairs={{0,4},{1,5},{2,6},{3,7},{4,0},{5,1},{6,2},{7,3},{8,12},{9,13},{10,... | collective-permute-start | bytes 208904 | tf_op jit(solution)/shard_map/ppermute | solution.py:312
  48.3 12.4 %collective-permute-start.12 = (bf16[272,128]{1,0:T(8,128)(2,1)S(1)}, bf16[272,128]{1,0:T(8,128)(2,1)S(1)}, u32[]{:S(2)}, u32[]{:S(2)}) collective-permute-start(bf16[272,128]{1,0:T(8,128)(2,1)S(1)} %get-tuple-element.81), channel_id=1, source_target_pairs={{0,5},{1,6},{2,7},{3,0},{4,1},{5,2},{6,3},{7,4},{8,13},{9,14},{10,... | collective-permute-start | bytes 208904 | tf_op jit(solution)/shard_map/ppermute | solution.py:312
  51.1 9.5 %collective-permute-start.13 = (bf16[272,128]{1,0:T(8,128)(2,1)S(1)}, bf16[272,128]{1,0:T(8,128)(2,1)S(1)}, u32[]{:S(2)}, u32[]{:S(2)}) collective-permute-start(bf16[272,128]{1,0:T(8,128)(2,1)S(1)} %get-tuple-element.82), channel_id=1, source_target_pairs={{0,3},{1,4},{2,5},{3,6},{4,7},{5,0},{6,1},{7,2},{8,11},{9,12},{10,... | collective-permute-start | bytes 208904 | tf_op jit(solution)/shard_map/ppermute | solution.py:312
  52.7 8.0 %collective-permute-start.14 = (bf16[272,128]{1,0:T(8,128)(2,1)S(1)}, bf16[272,128]{1,0:T(8,128)(2,1)S(1)}, u32[]{:S(2)}, u32[]{:S(2)}) collective-permute-start(bf16[272,128]{1,0:T(8,128)(2,1)S(1)} %get-tuple-element.83), channel_id=1, source_target_pairs={{0,6},{1,7},{2,0},{3,1},{4,2},{5,3},{6,4},{7,5},{8,14},{9,15},{10,... | collective-permute-start | bytes 208904 | tf_op jit(solution)/shard_map/ppermute | solution.py:312
  56.7 7.0 %collective-permute-start.15 = (bf16[272,128]{1,0:T(8,128)(2,1)S(1)}, bf16[272,128]{1,0:T(8,128)(2,1)S(1)}, u32[]{:S(2)}, u32[]{:S(2)}) collective-permute-start(bf16[272,128]{1,0:T(8,128)(2,1)S(1)} %get-tuple-element.84), channel_id=1, source_target_pairs={{0,2},{1,3},{2,4},{3,5},{4,6},{5,7},{6,0},{7,1},{8,10},{9,11},{10,... | collective-permute-start | bytes 208904 | tf_op jit(solution)/shard_map/ppermute | solution.py:312
  56.7 7.0 %collective-permute-start.16 = (bf16[272,128]{1,0:T(8,128)(2,1)S(1)}, bf16[272,128]{1,0:T(8,128)(2,1)S(1)}, u32[]{:S(2)}, u32[]{:S(2)}) collective-permute-start(bf16[272,128]{1,0:T(8,128)(2,1)S(1)} %get-tuple-element.85), channel_id=1, source_target_pairs={{0,7},{1,0},{2,1},{3,2},{4,3},{5,4},{6,5},{7,6},{8,15},{9,8},{10,9... | collective-permute-start | bytes 208904 | tf_op jit(solution)/shard_map/ppermute | solution.py:312
  60.7 5.5 %collective-permute-start.17 = (bf16[272,128]{1,0:T(8,128)(2,1)S(1)}, bf16[272,128]{1,0:T(8,128)(2,1)S(1)}, u32[]{:S(2)}, u32[]{:S(2)}) collective-permute-start(bf16[272,128]{1,0:T(8,128)(2,1)S(1)} %get-tuple-element.86), channel_id=1, source_target_pairs={{0,1},{1,2},{2,3},{3,4},{4,5},{5,6},{6,7},{7,0},{8,9},{9,10},{10,1... | collective-permute-start | bytes 208904 | tf_op jit(solution)/shard_map/ppermute | solution.py:312
where the time goes:
time: 67.5 us; the launch traced here: 67.3 us
  starting transfers between devices  32.7 us (48%)
  Pallas kernels  18.1 us (27%)
  waiting for transfers between devices  13.7 us (20%)
  local copies, waits for them, and re-layouts  2.06 us (3%)
  between operations  0.76 us (1%)
    ppermute x15, starting transfers between devices, zshift(): lax.ppermute(x, 'ctx', [(i, i // zsize * zsize + (i % zsize + by) % zsize...  28.6 us
    pallas_call x5, Pallas kernels, attend(): pl.pallas_call(functools.partial(attend_kernel, blocks, len(arrays), zsiz...  13.2 us
    ppermute x15, waiting for transfers between devices, zshift(): lax.ppermute(x, 'ctx', [(i, i // zsize * zsize + (i % zsize + by) % zsize...  8.23 us
    ppermute x3, waiting for transfers between devices, xswap(): lax.ppermute(x, 'ctx', [(i, (i + zsize) % (2 * zsize)) for i in range(2 *...  5.5 us
    ppermute x3, starting transfers between devices, xswap(): lax.ppermute(x, 'ctx', [(i, (i + zsize) % (2 * zsize)) for i in range(2 *...  4.12 us
    pallas_call x1, Pallas kernels, prep(): pl.pallas_call(prep_kernel, out_shape=[jax.ShapeDtypeStruct(s, jnp.bfloat...  2.65 us
    unnamed x8, local copies, waits for them, and re-layouts  2.05 us
  transfers between devices with their start and end apart: 18, of which 6 were waited for; matrix products, arithmetic and copies ran while one was open for 0% of the time, Pallas kernels for 25%

commit v1 on v0

--- a/solution.py
+++ b/solution.py
@@ -41,48 +41,59 @@
     return tile.astype(jnp.bfloat16)
 
 
-def prep_kernel(device_ref, length_ref, table_ref, k_hbm, v_hbm, nk_ref, nv_ref, k_out, v_out, live_out, nk_out, nv_out, k_ref, v_ref, sems):
-    pages = k_ref.shape[0] // PAGE
-    pieces = sems.shape[0] // 2
-    size = k_ref.shape[0] // pieces
-    copies = []
-    for src, dst, base in ((v_hbm, v_ref, 0), (k_hbm, k_ref, pieces)):
-        for i in range(pieces):
-            at = pl.ds(i * size, size)
-            copies.append(pltpu.make_async_copy(src.at[at], dst.at[at], sems.at[base + i]))
-            copies[-1].start()
-    entries = table_ref.shape[1]
+def live_pages(device_ref, meta_ref, pages):
+    entries = meta_ref.shape[1] - HD
+    length = meta_ref[:, entries:entries + 1]
     slot = lax.broadcasted_iota(jnp.int32, (pages, entries), 0) + device_ref[0] * pages
     index = lax.broadcasted_iota(jnp.int32, (pages, entries), 1)
-    hit = jnp.broadcast_to(table_ref[...], (pages, entries)) == slot
+    hit = jnp.broadcast_to(meta_ref[:, 0:entries], (pages, entries)) == slot
     logical = jnp.sum(jnp.where(hit, index, 0), axis=1, keepdims=True)
+    offset = lax.broadcasted_iota(jnp.int32, (PAGE, 1), 0)
+    return logical, length, lambda s: jnp.broadcast_to(logical[s:s + 1, :], (PAGE, 1)) * PAGE + offset < length
+
+
+def fetch(hbm, ref, sems):
+    size = ref.shape[0] // sems.shape[0]
+    copies = []
+    for i in range(sems.shape[0]):
+        at = pl.ds(i * size, size)
+        copies.append(pltpu.make_async_copy(hbm.at[at], ref.at[at], sems.at[i]))
+        copies[-1].start()
+    return copies
+
+
+def prep_keys_kernel(device_ref, meta_ref, new_ref, k_hbm, k_out, nk_out, nv_out, k_ref, sems):
+    copies = fetch(k_hbm, k_ref, sems)
+    pages = k_ref.shape[0] // PAGE
+    logical, length, live = live_pages(device_ref, meta_ref, pages)
     first = jnp.min(logical, axis=0, keepdims=True)
-    offset = lax.broadcasted_iota(jnp.int32, (PAGE, 1), 0)
     nk_out[...] = jnp.zeros_like(nk_out)
     nv_out[...] = jnp.zeros_like(nv_out)
-    nk_out[0:ROWS, :] = nk_ref[...]
-    nv_out[0:ROWS, :] = nv_ref[...]
-
-    def live_of(s):
-        return jnp.broadcast_to(logical[s:s + 1, :], (PAGE, 1)) * PAGE + offset < length_ref[0]
-
-    for s in range(pages):
-        if s % (pages // pieces) == 0:
-            copies[s // (pages // pieces)].wait()
-        rows = slice(s * PAGE, (s + 1) * PAGE)
-        live = live_of(s)
-        v_out[rows, :] = jnp.where(live, v_ref[rows, :].astype(jnp.float32), 0.0).astype(jnp.bfloat16)
-        live_out[rows, :] = jnp.broadcast_to(jnp.where(live, 1.0, 0.0), (PAGE, HD)).astype(jnp.bfloat16)
-    for copy in copies[pieces:]:
+    nk_out[0:ROWS, :] = new_ref[0:ROWS, :]
+    nv_out[0:ROWS, :] = new_ref[ROWS:2 * ROWS, :]
+    spare = new_ref[0:1, :].astype(jnp.float32)
+    for copy in copies:
         copy.wait()
-    spare = nk_ref[0:1, :].astype(jnp.float32)
     for s in range(pages):
         mine = logical[s:s + 1, :]
-        use = (mine == first) & (mine * PAGE < length_ref[0])
+        use = (mine == first) & (mine * PAGE < length)
         spare = jnp.where(use, k_ref[s * PAGE:s * PAGE + 1, :].astype(jnp.float32), spare)
     for s in range(pages):
         rows = slice(s * PAGE, (s + 1) * PAGE)
-        k_out[rows, :] = jnp.where(live_of(s), k_ref[rows, :].astype(jnp.float32), spare).astype(jnp.bfloat16)
+        k_out[rows, :] = jnp.where(live(s), k_ref[rows, :].astype(jnp.float32), spare).astype(jnp.bfloat16)
+
+
+def prep_values_kernel(device_ref, meta_ref, v_hbm, v_out, live_out, v_ref, sems):
+    copies = fetch(v_hbm, v_ref, sems)
+    pages = v_ref.shape[0] // PAGE
+    _, _, live = live_pages(device_ref, meta_ref, pages)
+    for s in range(pages):
+        if s % (pages // len(copies)) == 0:
+            copies[s // (pages // len(copies))].wait()
+        rows = slice(s * PAGE, (s + 1) * PAGE)
+        ok = live(s)
+        v_out[rows, :] = jnp.where(ok, v_ref[rows, :].astype(jnp.float32), 0.0).astype(jnp.bfloat16)
+        live_out[rows, :] = jnp.broadcast_to(jnp.where(ok, 1.0, 0.0), (PAGE, HD)).astype(jnp.bfloat16)
 
 
 def attend_kernel(blocks, nin, zsize, device_ref, *refs):
@@ -189,20 +200,16 @@
     return pltpu.CompilerParams(vmem_limit_bytes=mib << 20)
 
 
-def prep(device, length, table, k, v, nk, nv):
-    keys = k.shape[0]
-    shapes = [k.shape, v.shape, (keys, HD), (NEWPAD, KVH * HD), (NEWPAD, KVH * HD)]
-    hbm = pl.BlockSpec(memory_space=pltpu.HBM)
+def prep(kernel, device, small, big, shapes, mib):
     return pl.pallas_call(
-        prep_kernel,
+        kernel,
         out_shape=[jax.ShapeDtypeStruct(s, jnp.bfloat16) for s in shapes],
-        in_specs=[SM, SM, VM, hbm, hbm, VM, VM],
-        out_specs=[VM] * 5,
-        scratch_shapes=[pltpu.VMEM(k.shape, jnp.bfloat16), pltpu.VMEM(v.shape, jnp.bfloat16), pltpu.SemaphoreType.DMA((8,))],
-        compiler_params=limit(48),
-        cost_estimate=pl.CostEstimate(flops=4 * keys * KVH * HD, bytes_accessed=8 * keys * KVH * HD, transcendentals=0),
-        name="prep",
-    )(device, length, table, k, v, nk, nv)
+        in_specs=[SM] + [VM] * len(small) + [pl.BlockSpec(memory_space=pltpu.HBM)],
+        out_specs=[VM] * len(shapes),
+        scratch_shapes=[pltpu.VMEM(big.shape, jnp.bfloat16), pltpu.SemaphoreType.DMA((4,))],
+        compiler_params=limit(mib),
+        cost_estimate=pl.CostEstimate(flops=4 * big.size, bytes_accessed=4 * big.size, transcendentals=0),
+    )(device, *small, big)
 
 
 def attend(zsize, device, arrays, blocks, store, total, before=None):
@@ -244,11 +251,13 @@
 
 
 def pair_kernel(counts, own, *refs):
-    keeps, got_ref, outs = refs[:len(counts)], refs[len(counts)], refs[len(counts) + 1:]
-    places = [(keep, i) for keep, n in zip(keeps, counts) for i in range(n)]
+    kept, got = counts
+    keeps, gots, outs = refs[:len(kept)], refs[len(kept):len(kept) + len(got)], refs[len(kept) + len(got):]
+    places = [(keep, i) for keep, n in zip(keeps, kept) for i in range(n)]
+    theirs_at = [ref.at[i] for ref, n in zip(gots, got) for i in range(n)]
     rows, lses = [], []
     for p, (keep, i) in enumerate(places):
-        theirs = lse_rows(got_ref.at[p])
+        theirs = lse_rows(theirs_at[p])
         lses.append([])
         for j in range(2):
             w, lse = shares([keep[i, BLOCK + j:BLOCK + j + 1, :], theirs[j]])
@@ -258,7 +267,7 @@
     for p, (keep, i) in enumerate(places):
         for j in range(2):
             at, c = slice(j * HD, (j + 1) * HD), 4 * p + 2 * j
-            acc = cols[:, c:c + 1] * keep[i, at, :] + cols[:, c + 1:c + 2] * got_ref[p, at, :].astype(jnp.float32)
+            acc = cols[:, c:c + 1] * keep[i, at, :] + cols[:, c + 1:c + 2] * theirs_at[p][at, :].astype(jnp.float32)
             outs[p][at, :] = acc.astype(outs[p].dtype)
             if own and p == 0:
                 outs[p][BLOCK + j:BLOCK + j + 1, :] = lses[p][j]
@@ -266,18 +275,18 @@
             outs[p][BLOCK:PAYLOAD, :] = lse_tile(lses[p])
 
 
-def pair(keeps, got, own):
-    counts = [k.shape[0] for k in keeps]
-    shapes = [jax.ShapeDtypeStruct((PAYLOAD, HD), jnp.bfloat16)] * sum(counts)
+def pair(keeps, gots, own=False):
+    counts = [k.shape[0] for k in keeps], [g.shape[0] for g in gots]
+    shapes = [jax.ShapeDtypeStruct((PAYLOAD, HD), jnp.bfloat16)] * sum(counts[0])
     if own:
         shapes[0] = jax.ShapeDtypeStruct((KEPT, HD), jnp.float32)
     return pl.pallas_call(
         functools.partial(pair_kernel, counts, own),
         out_shape=shapes,
-        in_specs=[VM] * (len(keeps) + 1),
+        in_specs=[VM] * (len(keeps) + len(gots)),
         out_specs=[VM] * len(shapes),
         compiler_params=limit(4),
-    )(*keeps, got)
+    )(*keeps, *gots)
 
 
 def final_kernel(n, own_ref, *refs):
@@ -319,30 +328,36 @@
 
     device = lax.axis_index("ctx").astype(jnp.int32).reshape(1)
     mine = queries.reshape(ROWS, KVH * GROUP, HD).transpose(1, 0, 2).reshape(BLOCK, HD)
-    store = prep(device, cache_length, page_table.reshape(1, -1), cache_keys, cache_values, new_keys, new_values)
-    swapped, store = lax.optimization_barrier((xswap(mine), store))
+    entries = page_table.shape[0]
+    meta = jnp.where(lax.iota(jnp.int32, entries + HD) < entries, jnp.pad(page_table, (0, HD)), cache_length[0]).reshape(1, -1)
+    new = jnp.concatenate([new_keys, new_values])
+    small = (NEWPAD, KVH * HD)
+    keys, nk, nv = prep(prep_keys_kernel, device, [meta, new], cache_keys, [cache_keys.shape, small, small], 50)
+    swapped, keys = lax.optimization_barrier((xswap(mine), keys))
+    values, live = prep(prep_values_kernel, device, [meta], cache_values, [cache_values.shape, (cache_values.shape[0], HD)], 48)
+    store = (keys, values, live, nk, nv)
     both = jnp.stack([mine, swapped])
 
-    near = 2 * half - 3
     run = functools.partial(attend, zsize, device)
-    keeps = []
-    keep, send = run([both], [((0, w), 0, (w, 0)) for w in range(2)], store, near)
+    up, down = both, both
+    keeps, gots = [], []
+    keep, send = run([both], [((0, w), 0, (w, 0)) for w in range(2)], store, 3)
     keeps.append(keep)
-    up, down = both, both
-    for k in range(1, half - 1):
+    for k in range(1, half):
         up, down, send = lax.optimization_barrier((zshift(up, 1), zshift(down, -1), send))
-        keep, send = run([up, down], blocks_at(k, 2 * k - 1), store, near, send)
+        if k == half - 1:
+            far = zshift(up, 1)
+        keep, send = run([up, down], blocks_at(k, 1 if k == 1 else 0), store, 3 if k == 1 else 2, send if k == 1 else None)
         keeps.append(keep)
-    up, down, send = lax.optimization_barrier((zshift(up, 1), zshift(down, -1), send))
-    far = (zshift(up[0:1], 1), zshift(down[1:2], -1))
-    far_keep, far_send = run([up, down], blocks_at(half - 1, 0), store, 3)
-    far, far_send = lax.optimization_barrier((far, far_send))
-    last_keep, far_send = run(list(far), [((0, 0), 0, (0, half)), ((1, 0), 2, (1, half))], store, 3, far_send)
-
-    got, far_got = xswap(send), xswap(far_send)
-    own, *out = pair(keeps, got, True)
-    far_out = pair([far_keep, last_keep], far_got, False)
-    back = [zshift(far_out[2], half), zshift(far_out[0], 1 - half), zshift(far_out[1], half - 1)]
+        gots.append(xswap(send))
+    far, send = lax.optimization_barrier((far, send))
+    last_keep, send = run([far], [((0, w), 0, (w, half)) for w in range(2)], store, 1)
+    last_got = xswap(send)
+
+    third = pair(keeps[-1:], gots[-1:])
+    own, *out = pair(keeps[:-1], gots[:-1], True)
+    fourth = pair([last_keep], [last_got])
+    back = [zshift(fourth[0], half), zshift(third[0], 1 - half), zshift(third[1], half - 1)]
     for k in range(half - 2, 0, -1):
         back += [zshift(out[2 * k - 2], -k), zshift(out[2 * k - 1], k)]
     out = final(own, back)

time: 67.5 us -> 62.9 us (0.932); the launches traced: 67.3 us -> 61.9 us
  waiting for transfers between devices: 13.7 us -> 10.2 us
  starting transfers between devices: 32.7 us -> 30.4 us
  local copies, waits for them, and re-layouts: 2.06 us -> 0.01 us
  other arithmetic: 0.02 us -> 1.41 us
  Pallas kernels: 18.1 us -> 19 us
    ppermute x3 -> x5, waiting for transfers between devices: 5.5 us -> 0.01 us  [xswap(): lax.ppermute(x, 'ctx', [(i, (i + zsize) % (2 * zsize)) for i in range(2 *...]
    ppermute x15 -> x14, starting transfers between devices: 28.6 us -> 23.8 us  [zshift(): lax.ppermute(x, 'ctx', [(i, i // zsize * zsize + (i % zsize + by) % zsize...]
    ppermute x3 -> x5, starting transfers between devices: 4.12 us -> 6.55 us  [xswap(): lax.ppermute(x, 'ctx', [(i, (i + zsize) % (2 * zsize)) for i in range(2 *...]
    unnamed x8 -> x4, local copies, waits for them, and re-layouts: 2.05 us -> 0.01 us
    ppermute x15 -> x14, waiting for transfers between devices: 8.23 us -> 10.2 us  [zshift(): lax.ppermute(x, 'ctx', [(i, i // zsize * zsize + (i % zsize + by) % zsize...]
    concatenate x0 -> x1, other arithmetic: none -> 0.71 us  [local(): new = jnp.concatenate([new_keys, new_values])]
    select_n x0 -> x1, other arithmetic: none -> 0.68 us  [local(): jnp.where(lax.iota(jnp.int32, entries + HD) < entries, jnp.pad(page_table...]
    pallas_call x1 -> x2, Pallas kernels: 2.65 us -> 3.13 us  [prep(): pl.pallas_call(kernel, out_shape=[jax.ShapeDtypeStruct(s, jnp.bfloat16) f...]
  transfers between devices with their start and end apart: 18 -> 19, of which waited for: 6 -> 7; matrix products, arithmetic and copies ran while one was open for 0% -> 2% of each run, Pallas kernels for 25% -> 29%
where the time goes in v1:
time: 62.9 us; the launch traced here: 61.9 us
  starting transfers between devices  30.4 us (48%)
  Pallas kernels  19 us (30%)
  waiting for transfers between devices  10.2 us (16%)
  other arithmetic  1.41 us (2%)
  between operations  0.81 us (1%)
    ppermute x14, starting transfers between devices, zshift(): lax.ppermute(x, 'ctx', [(i, i // zsize * zsize + (i % zsize + by) % zsize...  23.8 us
    pallas_call x5, Pallas kernels, attend(): pl.pallas_call(functools.partial(attend_kernel, blocks, len(arrays), zsiz...  13.5 us
    ppermute x14, waiting for transfers between devices, zshift(): lax.ppermute(x, 'ctx', [(i, i // zsize * zsize + (i % zsize + by) % zsize...  10.2 us
    ppermute x5, starting transfers between devices, xswap(): lax.ppermute(x, 'ctx', [(i, (i + zsize) % (2 * zsize)) for i in range(2 *...  6.55 us
    pallas_call x2, Pallas kernels, prep(): pl.pallas_call(kernel, out_shape=[jax.ShapeDtypeStruct(s, jnp.bfloat16) f...  3.13 us
  transfers between devices with their start and end apart: 19, of which 7 were waited for; matrix products, arithmetic and copies ran while one was open for 2% of the time, Pallas kernels for 29%

profile of v1, /device:TPU:2, one launch (start us, length us, event | category | flops | bytes accessed | tf_op | source)
XLA Modules:
  0.0 61.9 jit_solution(12978470901642944436)
XLA Ops:
  0.0 2.2 %collective-permute-start = (bf16[256,128]{1,0:T(8,128)(2,1)}, bf16[256,128]{1,0:T(8,128)(2,1)S(1)}, u32[]{:S(2)}, u32[]{:S(2)}) collective-permute-start(bf16[256,128]{1,0:T(8,128)(2,1)} %bitcast.16), channel_id=1, source_target_pairs={{0,8},{1,9},{2,10},{3,11},{4,12},{5,13},{6,14},{7,15},{8,0},{9,1},... | collective-permute-start | bytes 196616 | tf_op jit(solution)/shard_map/ppermute | solution.py:324
  4.3 2.1 %shard_map.73 = (bf16[2048,512]{1,0:T(8,128)(2,1)S(1)}, bf16[16,512]{1,0:T(8,128)(2,1)S(1)}, bf16[16,512]{1,0:T(8,128)(2,1)S(1)}) custom-call(s32[1]{0:T(128)} %bitcast.device_ref, s32[1,384]{1,0:T(1,128)S(1)} %reshape.21.meta_ref, bf16[8,512]{1,0:T(8,128)(2,1)S(1)} %pad_maximum_fusion.1.new_ref, bf16[2048,512]{1,0:T(8,128)(2,1)} %k_hbm.1), custom_call_target="tpu_custom_call" | custom-call | flops 4194304 | bytes 4194304 | tf_op jit(solution)/shard_map/pallas_call | solution.py:204
  6.5 4.3 %collective-permute-start.2 = (bf16[2,256,128]{2,1,0:T(8,128)(2,1)S(1)}, bf16[2,256,128]{2,1,0:T(8,128)(2,1)S(1)}, u32[]{:S(2)}, u32[]{:S(2)}) collective-permute-start(bf16[2,256,128]{2,1,0:T(8,128)(2,1)S(1)} %pad_maximum_fusion.refs_0_), channel_id=1, source_target_pairs={{0,7},{1,0},{2,1},{3,2},{4,3},{5,4},{6,5},{7,6},{8,15},{9,8},{10,9... | collective-permute-start | bytes 393224 | tf_op jit(solution)/shard_map/ppermute | solution.py:321
  10.8 1.0 %shard_map.74 = (bf16[2048,512]{1,0:T(8,128)(2,1)S(1)}, bf16[2048,128]{1,0:T(8,128)(2,1)S(1)}) custom-call(s32[1]{0:T(128)} %bitcast.device_ref, s32[1,384]{1,0:T(1,128)S(1)} %reshape.21.meta_ref, bf16[2048,512]{1,0:T(8,128)(2,1)S(1)} %copy-done), custom_call_target="tpu_custom_call" | custom-call | flops 4194304 | bytes 4194304 | tf_op jit(solution)/shard_map/pallas_call | solution.py:204
  11.8 2.3 %shard_map.75 = (f32[1,264,128]{2,1,0:T(8,128)S(1)}, bf16[3,272,128]{2,1,0:T(8,128)(2,1)S(1)}) custom-call(s32[1]{0:T(128)} %bitcast.device_ref, bf16[2,256,128]{2,1,0:T(8,128)(2,1)S(1)} %pad_maximum_fusion.refs_0_, bf16[2048,512]{1,0:T(8,128)(2,1)S(1)} %get-tuple-element.39.refs_1_.refs_2_, bf16[2048,512]{1,0:T(8,128)(2,1)S(1)} %get-tuple-element.40.refs_2_.refs_3_, ...), custom_call_target="tpu_custom_call" | custom-call | flops 536870912 | bytes 4194304 | tf_op jit(solution)/shard_map/pallas_call | solution.py:220
  14.1 2.8 %collective-permute-done.1.refs_0_ = bf16[2,256,128]{2,1,0:T(8,128)(2,1)S(1)} collective-permute-done((bf16[2,256,128]{2,1,0:T(8,128)(2,1)S(1)}, bf16[2,256,128]{2,1,0:T(8,128)(2,1)S(1)}, u32[]{:S(2)}, u32[]{:S(2)}) %collective-permute-start.1) | collective-permute-done | bytes 131104 | tf_op jit(solution)/shard_map/ppermute | solution.py:321
  17.0 3.2 %collective-permute-start.4 = (bf16[2,256,128]{2,1,0:T(8,128)(2,1)S(1)}, bf16[2,256,128]{2,1,0:T(8,128)(2,1)S(1)}, u32[]{:S(2)}, u32[]{:S(2)}) collective-permute-start(bf16[2,256,128]{2,1,0:T(8,128)(2,1)S(1)} %collective-permute-done.2.refs_1_), channel_id=1, source_target_pairs={{0,7},{1,0},{2,1},{3,2},{4,3},{5,4},{6,5},{7,6},{8,15},{9,8},{10,9... | collective-permute-start | bytes 393224 | tf_op jit(solution)/shard_map/ppermute | solution.py:321
  20.2 3.0 %shard_map.76 = (f32[2,264,128]{2,1,0:T(8,128)S(1)}, bf16[3,272,128]{2,1,0:T(8,128)(2,1)S(1)}) custom-call(s32[1]{0:T(128)} %bitcast.device_ref, bf16[2,256,128]{2,1,0:T(8,128)(2,1)S(1)} %collective-permute-done.1.refs_0_, bf16[2,256,128]{2,1,0:T(8,128)(2,1)S(1)} %collective-permute-done.2.refs_1_, ...), custom_call_target="tpu_custom_call", output_to_operand_aliasing={{1}: (8, {})} | custom-call | flops 1073741824 | bytes 4194304 | tf_op jit(solution)/shard_map/pallas_call | solution.py:220
  23.3 3.2 %collective-permute-start.8 = (bf16[2,256,128]{2,1,0:T(8,128)(2,1)S(1)}, bf16[2,256,128]{2,1,0:T(8,128)(2,1)S(1)}, u32[]{:S(2)}, u32[]{:S(2)}) collective-permute-start(bf16[2,256,128]{2,1,0:T(8,128)(2,1)S(1)} %collective-permute-done.4.refs_1_), channel_id=1, source_target_pairs={{0,7},{1,0},{2,1},{3,2},{4,3},{5,4},{6,5},{7,6},{8,15},{9,8},{10,9... | collective-permute-start | bytes 393224 | tf_op jit(solution)/shard_map/ppermute | solution.py:321
  26.5 1.4 %collective-permute-start.5 = (bf16[3,272,128]{2,1,0:T(8,128)(2,1)S(1)}, bf16[3,272,128]{2,1,0:T(8,128)(2,1)S(1)}, u32[]{:S(2)}, u32[]{:S(2)}) collective-permute-start(bf16[3,272,128]{2,1,0:T(8,128)(2,1)S(1)} %get-tuple-element.50), channel_id=1, source_target_pairs={{0,8},{1,9},{2,10},{3,11},{4,12},{5,13},{6,14},{7,15},{8,0},{9,1},... | collective-permute-start | bytes 626696 | tf_op jit(solution)/shard_map/ppermute | solution.py:324
  27.9 3.0 %shard_map.77 = (f32[2,264,128]{2,1,0:T(8,128)S(1)}, bf16[2,272,128]{2,1,0:T(8,128)(2,1)S(1)}) custom-call(s32[1]{0:T(128)} %bitcast.device_ref, bf16[2,256,128]{2,1,0:T(8,128)(2,1)S(1)} %collective-permute-done.3.refs_0_, bf16[2,256,128]{2,1,0:T(8,128)(2,1)S(1)} %collective-permute-done.4.refs_1_, bf16[2048,512]{1,0:T(8,128)(2,1)S(1)} %get-tuple-element.39.refs_1_.refs_2_, ...), custom_call_target="tpu_custom_call" | custom-call | flops 1073741824 | bytes 4194304 | tf_op jit(solution)/shard_map/pallas_call | solution.py:220
  31.8 3.0 %shard_map.79 = (f32[2,264,128]{2,1,0:T(8,128)S(1)}, bf16[2,272,128]{2,1,0:T(8,128)(2,1)S(1)}) custom-call(s32[1]{0:T(128)} %bitcast.device_ref, bf16[2,256,128]{2,1,0:T(8,128)(2,1)S(1)} %collective-permute-done.7.refs_0_, bf16[2,256,128]{2,1,0:T(8,128)(2,1)S(1)} %collective-permute-done.8.refs_1_, bf16[2048,512]{1,0:T(8,128)(2,1)S(1)} %get-tuple-element.39.refs_1_.refs_2_, ...), custom_call_target="tpu_custom_call" | custom-call | flops 1073741824 | bytes 4194304 | tf_op jit(solution)/shard_map/pallas_call | solution.py:220
  34.8 1.5 %collective-permute-start.12 = (bf16[2,272,128]{2,1,0:T(8,128)(2,1)S(1)}, bf16[2,272,128]{2,1,0:T(8,128)(2,1)S(1)}, u32[]{:S(2)}, u32[]{:S(2)}) collective-permute-start(bf16[2,272,128]{2,1,0:T(8,128)(2,1)S(1)} %get-tuple-element.58), channel_id=1, source_target_pairs={{0,8},{1,9},{2,10},{3,11},{4,12},{5,13},{6,14},{7,15},{8,0},{9,1},... | collective-permute-start | bytes 417800 | tf_op jit(solution)/shard_map/ppermute | solution.py:324
  36.2 1.0 %collective-permute-done.9.refs_0_ = bf16[2,256,128]{2,1,0:T(8,128)(2,1)S(1)} collective-permute-done((bf16[2,256,128]{2,1,0:T(8,128)(2,1)S(1)}, bf16[2,256,128]{2,1,0:T(8,128)(2,1)S(1)}, u32[]{:S(2)}, u32[]{:S(2)}) %collective-permute-start.9) | collective-permute-done | bytes 131104 | tf_op jit(solution)/shard_map/ppermute | solution.py:321
  37.2 2.3 %shard_map.80 = (f32[1,264,128]{2,1,0:T(8,128)S(1)}, bf16[1,272,128]{2,1,0:T(8,128)(2,1)S(1)}) custom-call(s32[1]{0:T(128)} %bitcast.device_ref, bf16[2,256,128]{2,1,0:T(8,128)(2,1)S(1)} %collective-permute-done.9.refs_0_, bf16[2048,512]{1,0:T(8,128)(2,1)S(1)} %get-tuple-element.39.refs_1_.refs_2_, bf16[2048,512]{1,0:T(8,128)(2,1)S(1)} %get-tuple-element.40.refs_2_.refs_3_, ...), custom_call_target="tpu_custom_call" | custom-call | flops 536870912 | bytes 4194304 | tf_op jit(solution)/shard_map/pallas_call | solution.py:220
  40.8 2.9 %collective-permute-start.15 = (bf16[272,128]{1,0:T(8,128)(2,1)S(1)}, bf16[272,128]{1,0:T(8,128)(2,1)S(1)}, u32[]{:S(2)}, u32[]{:S(2)}) collective-permute-start(bf16[272,128]{1,0:T(8,128)(2,1)S(1)} %get-tuple-element.65), channel_id=1, source_target_pairs={{0,6},{1,7},{2,0},{3,1},{4,2},{5,3},{6,4},{7,5},{8,14},{9,15},{10,... | collective-permute-start | bytes 208904 | tf_op jit(solution)/shard_map/ppermute | solution.py:321
  43.8 3.4 %collective-permute-start.17 = (bf16[272,128]{1,0:T(8,128)(2,1)S(1)}, bf16[272,128]{1,0:T(8,128)(2,1)S(1)}, u32[]{:S(2)}, u32[]{:S(2)}) collective-permute-start(bf16[272,128]{1,0:T(8,128)(2,1)S(1)} %get-tuple-element.67), channel_id=1, source_target_pairs={{0,7},{1,0},{2,1},{3,2},{4,3},{5,4},{6,5},{7,6},{8,15},{9,8},{10,9... | collective-permute-start | bytes 208904 | tf_op jit(solution)/shard_map/ppermute | solution.py:321
  47.6 2.2 %collective-permute-start.13 = (bf16[272,128]{1,0:T(8,128)(2,1)S(1)}, bf16[272,128]{1,0:T(8,128)(2,1)S(1)}, u32[]{:S(2)}, u32[]{:S(2)}) collective-permute-start(bf16[272,128]{1,0:T(8,128)(2,1)S(1)} %get-tuple-element.63), channel_id=1, source_target_pairs={{0,5},{1,6},{2,7},{3,0},{4,1},{5,2},{6,3},{7,4},{8,13},{9,14},{10,... | collective-permute-start | bytes 208904 | tf_op jit(solution)/shard_map/ppermute | solution.py:321
  50.1 1.8 %collective-permute-start.14 = (bf16[272,128]{1,0:T(8,128)(2,1)S(1)}, bf16[272,128]{1,0:T(8,128)(2,1)S(1)}, u32[]{:S(2)}, u32[]{:S(2)}) collective-permute-start(bf16[272,128]{1,0:T(8,128)(2,1)S(1)} %get-tuple-element.64), channel_id=1, source_target_pairs={{0,3},{1,4},{2,5},{3,6},{4,7},{5,0},{6,1},{7,2},{8,11},{9,12},{10,... | collective-permute-start | bytes 208904 | tf_op jit(solution)/shard_map/ppermute | solution.py:321
  52.1 2.5 %collective-permute-start.11 = (bf16[272,128]{1,0:T(8,128)(2,1)S(1)}, bf16[272,128]{1,0:T(8,128)(2,1)S(1)}, u32[]{:S(2)}, u32[]{:S(2)}) collective-permute-start(bf16[272,128]{1,0:T(8,128)(2,1)S(1)} %shard_map.81), channel_id=1, source_target_pairs={{0,4},{1,5},{2,6},{3,7},{4,0},{5,1},{6,2},{7,3},{8,12},{9,13},{10,... | collective-permute-start | bytes 208904 | tf_op jit(solution)/shard_map/ppermute | solution.py:321
  55.0 1.3 %collective-permute-done.13.refs_1_ = bf16[272,128]{1,0:T(8,128)(2,1)S(1)} collective-permute-done((bf16[272,128]{1,0:T(8,128)(2,1)S(1)}, bf16[272,128]{1,0:T(8,128)(2,1)S(1)}, u32[]{:S(2)}, u32[]{:S(2)}) %collective-permute-start.13) | collective-permute-done | bytes 69664 | tf_op jit(solution)/shard_map/ppermute | solution.py:321
  56.3 1.6 %collective-permute-done.14.refs_2_ = bf16[272,128]{1,0:T(8,128)(2,1)S(1)} collective-permute-done((bf16[272,128]{1,0:T(8,128)(2,1)S(1)}, bf16[272,128]{1,0:T(8,128)(2,1)S(1)}, u32[]{:S(2)}, u32[]{:S(2)}) %collective-permute-start.14) | collective-permute-done | bytes 69664 | tf_op jit(solution)/shard_map/ppermute | solution.py:321
  57.9 2.8 %collective-permute-done.11.refs_0_ = bf16[272,128]{1,0:T(8,128)(2,1)S(1)} collective-permute-done((bf16[272,128]{1,0:T(8,128)(2,1)S(1)}, bf16[272,128]{1,0:T(8,128)(2,1)S(1)}, u32[]{:S(2)}, u32[]{:S(2)}) %collective-permute-start.11) | collective-permute-done | bytes 69664 | tf_op jit(solution)/shard_map/ppermute | solution.py:321
  60.7 1.1 %final.1 = bf16[256,128]{1,0:T(8,128)(2,1)} custom-call(f32[264,128]{1,0:T(8,128)S(1)} %get-tuple-element.55.own_ref, bf16[272,128]{1,0:T(8,128)(2,1)S(1)} %collective-permute-done.11.refs_0_, bf16[272,128]{1,0:T(8,128)(2,1)S(1)} %collective-permute-done.13.refs_1_, bf16[272,128]{1,0:T(8,128)(2,1)S(1)} %collective-permute-done.14.refs_2_, ...), custom_call_target="tpu_custom_call" | custom-call | tf_op jit(solution)/shard_map/final/pallas_call | solution.py:306
  (33 shorter events, 5.2 us)
Async XLA Ops:
  0.0 6.4 %copy-start.1 = (bf16[4,8192]{1,0:T(4,128)(2,1)S(1)}, bf16[4,8192]{1,0:T(4,128)(2,1)}, u32[]{:S(2)}) copy-start(bf16[4,8192]{1,0:T(4,128)(2,1)} %param.7) | copy-start | bytes 196612
  0.0 10.8 %copy-start = (bf16[2048,512]{1,0:T(8,128)(2,1)S(1)}, bf16[2048,512]{1,0:T(8,128)(2,1)}, u32[]{:S(2)}) copy-start(bf16[2048,512]{1,0:T(8,128)(2,1)} %v_hbm.1) | copy-start | bytes 6291460
  0.0 6.4 %collective-permute-start = (bf16[256,128]{1,0:T(8,128)(2,1)}, bf16[256,128]{1,0:T(8,128)(2,1)S(1)}, u32[]{:S(2)}, u32[]{:S(2)}) collective-permute-start(bf16[256,128]{1,0:T(8,128)(2,1)} %bitcast.16), channel_id=1, source_target_pairs={{0,8},{1,9},{2,10},{3,11},{4,12},{5,13},{6,14},{7,15},{8,0},{9,1},... | collective-permute-start | bytes 196616 | tf_op jit(solution)/shard_map/ppermute | solution.py:324
  6.5 7.7 %collective-permute-start.2 = (bf16[2,256,128]{2,1,0:T(8,128)(2,1)S(1)}, bf16[2,256,128]{2,1,0:T(8,128)(2,1)S(1)}, u32[]{:S(2)}, u32[]{:S(2)}) collective-permute-start(bf16[2,256,128]{2,1,0:T(8,128)(2,1)S(1)} %pad_maximum_fusion.refs_0_), channel_id=1, source_target_pairs={{0,7},{1,0},{2,1},{3,2},{4,3},{5,4},{6,5},{7,6},{8,15},{9,8},{10,9... | collective-permute-start | bytes 393224 | tf_op jit(solution)/shard_map/ppermute | solution.py:321
  10.8 6.2 %collective-permute-start.1 = (bf16[2,256,128]{2,1,0:T(8,128)(2,1)S(1)}, bf16[2,256,128]{2,1,0:T(8,128)(2,1)S(1)}, u32[]{:S(2)}, u32[]{:S(2)}) collective-permute-start(bf16[2,256,128]{2,1,0:T(8,128)(2,1)S(1)} %pad_maximum_fusion.refs_0_), channel_id=1, source_target_pairs={{0,1},{1,2},{2,3},{3,4},{4,5},{5,6},{6,7},{7,0},{8,9},{9,10},{10,1... | collective-permute-start | bytes 393224 | tf_op jit(solution)/shard_map/ppermute | solution.py:321
  17.0 6.2 %collective-permute-start.3 = (bf16[2,256,128]{2,1,0:T(8,128)(2,1)S(1)}, bf16[2,256,128]{2,1,0:T(8,128)(2,1)S(1)}, u32[]{:S(2)}, u32[]{:S(2)}) collective-permute-start(bf16[2,256,128]{2,1,0:T(8,128)(2,1)S(1)} %collective-permute-done.1.refs_0_), channel_id=1, source_target_pairs={{0,1},{1,2},{2,3},{3,4},{4,5},{5,6},{6,7},{7,0},{8,9},{9,10},{10,1... | collective-permute-start | bytes 393224 | tf_op jit(solution)/shard_map/ppermute | solution.py:321
  17.0 6.2 %collective-permute-start.4 = (bf16[2,256,128]{2,1,0:T(8,128)(2,1)S(1)}, bf16[2,256,128]{2,1,0:T(8,128)(2,1)S(1)}, u32[]{:S(2)}, u32[]{:S(2)}) collective-permute-start(bf16[2,256,128]{2,1,0:T(8,128)(2,1)S(1)} %collective-permute-done.2.refs_1_), channel_id=1, source_target_pairs={{0,7},{1,0},{2,1},{3,2},{4,3},{5,4},{6,5},{7,6},{8,15},{9,8},{10,9... | collective-permute-start | bytes 393224 | tf_op jit(solution)/shard_map/ppermute | solution.py:321
  23.2 7.7 %collective-permute-start.7 = (bf16[2,256,128]{2,1,0:T(8,128)(2,1)S(1)}, bf16[2,256,128]{2,1,0:T(8,128)(2,1)S(1)}, u32[]{:S(2)}, u32[]{:S(2)}) collective-permute-start(bf16[2,256,128]{2,1,0:T(8,128)(2,1)S(1)} %collective-permute-done.3.refs_0_), channel_id=1, source_target_pairs={{0,1},{1,2},{2,3},{3,4},{4,5},{5,6},{6,7},{7,0},{8,9},{9,10},{10,1... | collective-permute-start | bytes 393224 | tf_op jit(solution)/shard_map/ppermute | solution.py:321
  23.3 7.6 %collective-permute-start.8 = (bf16[2,256,128]{2,1,0:T(8,128)(2,1)S(1)}, bf16[2,256,128]{2,1,0:T(8,128)(2,1)S(1)}, u32[]{:S(2)}, u32[]{:S(2)}) collective-permute-start(bf16[2,256,128]{2,1,0:T(8,128)(2,1)S(1)} %collective-permute-done.4.refs_1_), channel_id=1, source_target_pairs={{0,7},{1,0},{2,1},{3,2},{4,3},{5,4},{6,5},{7,6},{8,15},{9,8},{10,9... | collective-permute-start | bytes 393224 | tf_op jit(solution)/shard_map/ppermute | solution.py:321
  26.5 13.7 %collective-permute-start.5 = (bf16[3,272,128]{2,1,0:T(8,128)(2,1)S(1)}, bf16[3,272,128]{2,1,0:T(8,128)(2,1)S(1)}, u32[]{:S(2)}, u32[]{:S(2)}) collective-permute-start(bf16[3,272,128]{2,1,0:T(8,128)(2,1)S(1)} %get-tuple-element.50), channel_id=1, source_target_pairs={{0,8},{1,9},{2,10},{3,11},{4,12},{5,13},{6,14},{7,15},{8,0},{9,1},... | collective-permute-start | bytes 626696 | tf_op jit(solution)/shard_map/ppermute | solution.py:324
  30.9 6.3 %collective-permute-start.9 = (bf16[2,256,128]{2,1,0:T(8,128)(2,1)S(1)}, bf16[2,256,128]{2,1,0:T(8,128)(2,1)S(1)}, u32[]{:S(2)}, u32[]{:S(2)}) collective-permute-start(bf16[2,256,128]{2,1,0:T(8,128)(2,1)S(1)} %collective-permute-done.7.refs_0_), channel_id=1, source_target_pairs={{0,1},{1,2},{2,3},{3,4},{4,5},{5,6},{6,7},{7,0},{8,9},{9,10},{10,1... | collective-permute-start | bytes 393224 | tf_op jit(solution)/shard_map/ppermute | solution.py:321
  31.0 9.2 %collective-permute-start.6 = (bf16[2,272,128]{2,1,0:T(8,128)(2,1)S(1)}, bf16[2,272,128]{2,1,0:T(8,128)(2,1)S(1)}, u32[]{:S(2)}, u32[]{:S(2)}) collective-permute-start(bf16[2,272,128]{2,1,0:T(8,128)(2,1)S(1)} %get-tuple-element.54), channel_id=1, source_target_pairs={{0,8},{1,9},{2,10},{3,11},{4,12},{5,13},{6,14},{7,15},{8,0},{9,1},... | collective-permute-start | bytes 417800 | tf_op jit(solution)/shard_map/ppermute | solution.py:324
  34.8 12.5 %collective-permute-start.12 = (bf16[2,272,128]{2,1,0:T(8,128)(2,1)S(1)}, bf16[2,272,128]{2,1,0:T(8,128)(2,1)S(1)}, u32[]{:S(2)}, u32[]{:S(2)}) collective-permute-start(bf16[2,272,128]{2,1,0:T(8,128)(2,1)S(1)} %get-tuple-element.58), channel_id=1, source_target_pairs={{0,8},{1,9},{2,10},{3,11},{4,12},{5,13},{6,14},{7,15},{8,0},{9,1},... | collective-permute-start | bytes 417800 | tf_op jit(solution)/shard_map/ppermute | solution.py:324
  39.5 8.1 %collective-permute-start.10 = (bf16[1,272,128]{2,1,0:T(8,128)(2,1)S(1)}, bf16[1,272,128]{2,1,0:T(8,128)(2,1)S(1)}, u32[]{:S(2)}, u32[]{:S(2)}) collective-permute-start(bf16[1,272,128]{2,1,0:T(8,128)(2,1)S(1)} %get-tuple-element.61), channel_id=1, source_target_pairs={{0,8},{1,9},{2,10},{3,11},{4,12},{5,13},{6,14},{7,15},{8,0},{9,1},... | collective-permute-start | bytes 208904 | tf_op jit(solution)/shard_map/ppermute | solution.py:324
  40.8 9.2 %collective-permute-start.15 = (bf16[272,128]{1,0:T(8,128)(2,1)S(1)}, bf16[272,128]{1,0:T(8,128)(2,1)S(1)}, u32[]{:S(2)}, u32[]{:S(2)}) collective-permute-start(bf16[272,128]{1,0:T(8,128)(2,1)S(1)} %get-tuple-element.65), channel_id=1, source_target_pairs={{0,6},{1,7},{2,0},{3,1},{4,2},{5,3},{6,4},{7,5},{8,14},{9,15},{10,... | collective-permute-start | bytes 208904 | tf_op jit(solution)/shard_map/ppermute | solution.py:321
  43.7 8.3 %collective-permute-start.16 = (bf16[272,128]{1,0:T(8,128)(2,1)S(1)}, bf16[272,128]{1,0:T(8,128)(2,1)S(1)}, u32[]{:S(2)}, u32[]{:S(2)}) collective-permute-start(bf16[272,128]{1,0:T(8,128)(2,1)S(1)} %get-tuple-element.66), channel_id=1, source_target_pairs={{0,2},{1,3},{2,4},{3,5},{4,6},{5,7},{6,0},{7,1},{8,10},{9,11},{10,... | collective-permute-start | bytes 208904 | tf_op jit(solution)/shard_map/ppermute | solution.py:321
  43.8 10.7 %collective-permute-start.17 = (bf16[272,128]{1,0:T(8,128)(2,1)S(1)}, bf16[272,128]{1,0:T(8,128)(2,1)S(1)}, u32[]{:S(2)}, u32[]{:S(2)}) collective-permute-start(bf16[272,128]{1,0:T(8,128)(2,1)S(1)} %get-tuple-element.67), channel_id=1, source_target_pairs={{0,7},{1,0},{2,1},{3,2},{4,3},{5,4},{6,5},{7,6},{8,15},{9,8},{10,9... | collective-permute-start | bytes 208904 | tf_op jit(solution)/shard_map/ppermute | solution.py:321
  47.2 7.8 %collective-permute-start.18 = (bf16[272,128]{1,0:T(8,128)(2,1)S(1)}, bf16[272,128]{1,0:T(8,128)(2,1)S(1)}, u32[]{:S(2)}, u32[]{:S(2)}) collective-permute-start(bf16[272,128]{1,0:T(8,128)(2,1)S(1)} %get-tuple-element.68), channel_id=1, source_target_pairs={{0,1},{1,2},{2,3},{3,4},{4,5},{5,6},{6,7},{7,0},{8,9},{9,10},{10,1... | collective-permute-start | bytes 208904 | tf_op jit(solution)/shard_map/ppermute | solution.py:321
  47.6 8.7 %collective-permute-start.13 = (bf16[272,128]{1,0:T(8,128)(2,1)S(1)}, bf16[272,128]{1,0:T(8,128)(2,1)S(1)}, u32[]{:S(2)}, u32[]{:S(2)}) collective-permute-start(bf16[272,128]{1,0:T(8,128)(2,1)S(1)} %get-tuple-element.63), channel_id=1, source_target_pairs={{0,5},{1,6},{2,7},{3,0},{4,1},{5,2},{6,3},{7,4},{8,13},{9,14},{10,... | collective-permute-start | bytes 208904 | tf_op jit(solution)/shard_map/ppermute | solution.py:321
  50.1 7.8 %collective-permute-start.14 = (bf16[272,128]{1,0:T(8,128)(2,1)S(1)}, bf16[272,128]{1,0:T(8,128)(2,1)S(1)}, u32[]{:S(2)}, u32[]{:S(2)}) collective-permute-start(bf16[272,128]{1,0:T(8,128)(2,1)S(1)} %get-tuple-element.64), channel_id=1, source_target_pairs={{0,3},{1,4},{2,5},{3,6},{4,7},{5,0},{6,1},{7,2},{8,11},{9,12},{10,... | collective-permute-start | bytes 208904 | tf_op jit(solution)/shard_map/ppermute | solution.py:321
  52.1 8.7 %collective-permute-start.11 = (bf16[272,128]{1,0:T(8,128)(2,1)S(1)}, bf16[272,128]{1,0:T(8,128)(2,1)S(1)}, u32[]{:S(2)}, u32[]{:S(2)}) collective-permute-start(bf16[272,128]{1,0:T(8,128)(2,1)S(1)} %shard_map.81), channel_id=1, source_target_pairs={{0,4},{1,5},{2,6},{3,7},{4,0},{5,1},{6,2},{7,3},{8,12},{9,13},{10,... | collective-permute-start | bytes 208904 | tf_op jit(solution)/shard_map/ppermute | solution.py:321
